TPU v7x, 512 devices: a whole 4x4x16 slice. The times are simulated.
512 devices in a mesh: head: 8 (over x, core), ctx: 64 (over y, z).
Axes of the slice: x: 4, y: 4, z: 16, core: 2. Of those that a mesh axis runs over, the one named last changes fastest.
Arguments:
- queries: bfloat16 [8, 64, 1024, 128], P('head', 'ctx'), may hold values from -72 to 72
- keys: bfloat16 [8, 262144, 128], P('head', 'ctx'), may hold values from -24 to 24
- values: bfloat16 [8, 262144, 128], P('head', 'ctx'), may hold values from -6 to 6
- kept: int32 [8, 512], P('head'), may hold values from 0 to 262143, as said below
- roots: int32 [8], P('head'), may hold values from 0 to 63
Outputs:
- compact: float32 [8, 512, 128], P('head')
- fit_error: float32 [], replicated
Inputs may be any that keep to these rules, and one draw needn't show every extreme that they name: `kept`: per head: 512 distinct increasing positions; at most 32 of them lie within one context device's 4096 positions, and exactly 32 within at least one such device.
All inputs are finite; a program needn't handle non-finite values.
Results may differ from a plain program's by a relative error of at most 0.0003.
Values may be sent and summed in bfloat16 or wider, within the bound.
A program may use at most 64 MiB of HBM per device.

v0:
```python
import math

import jax
import jax.numpy as jnp
from jax import lax
from jax.sharding import PartitionSpec as P

HD = 128
KBLK = 1024
M = 512


ridge_share = 0.01


def spread(array, axis, root):
    mine = lax.axis_index(axis) == root
    return lax.psum(jnp.where(mine, array, jnp.zeros_like(array)), axis)


def merge_parts(first, second):
    first_max, first_sum, first_out = first
    second_max, second_sum, second_out = second
    joint = jnp.maximum(first_max, second_max)
    first_scale = jnp.exp(first_max - joint)
    second_scale = jnp.exp(second_max - joint)
    return (
        joint,
        first_sum * first_scale + second_sum * second_scale,
        first_out * first_scale[:, None] + second_out * second_scale[:, None],
    )


def block_partials(queries_ref, key_slab, value_slab, score_scale):
    blocks = key_slab.shape[0] // KBLK
    key_blocks = key_slab.reshape(blocks, KBLK, HD)
    value_blocks = value_slab.reshape(blocks, KBLK, HD)
    rows = queries_ref.shape[0]

    def visit(carry, pieces):
        key_block, value_block = pieces
        scores = (
            jnp.einsum("rd,kd->rk", queries_ref, key_block, preferred_element_type=jnp.float32)
            * score_scale
        )
        block_max = jnp.max(scores, axis=1)
        weights = jnp.exp(scores - block_max[:, None]).astype(jnp.bfloat16)
        block_sum = jnp.sum(weights.astype(jnp.float32), axis=1)
        block_out = jnp.dot(weights, value_block, preferred_element_type=jnp.float32)
        return (merge_parts(carry, (block_max, block_sum, block_out)), None)

    start = (
        jnp.full((rows,), -jnp.inf, jnp.float32),
        jnp.zeros((rows,), jnp.float32),
        jnp.zeros((rows, HD), jnp.float32),
    )
    return lax.scan(visit, start, (key_blocks, value_blocks))[0]


def compact_softmax(queries_ref, compact_keys, score_scale):
    scores = (
        jnp.einsum("rd,md->rm", queries_ref, compact_keys, preferred_element_type=jnp.float32)
        * score_scale
    )
    return jax.nn.softmax(scores, axis=1)


def inner_left(left, right):
    return lax.dot_general(
        left,
        right,
        (((0,), (0,)), ((), ())),
        precision=lax.Precision.HIGHEST,
        preferred_element_type=jnp.float32,
    )


def per_device(queries, keys, values, kept, roots):
    score_scale = 1.0 / math.sqrt(HD)
    queries_ref = spread(queries[0, 0], "ctx", roots[0])
    run_max, run_sum, run_out = block_partials(queries_ref, keys[0], values[0], score_scale)
    highest = lax.pmax(run_max, "ctx")
    rescale = jnp.exp(run_max - highest)
    run_sum, run_out = lax.psum((run_sum * rescale, run_out * rescale[:, None]), "ctx")
    target = run_out / run_sum[:, None]
    slab = keys.shape[1]
    shard = lax.axis_index("ctx")
    positions = kept[0]
    owner = positions // slab
    local_rows = positions - shard * slab
    mine = owner == shard
    picked = jnp.take(keys[0], jnp.clip(local_rows, 0, slab - 1), axis=0).astype(jnp.float32)
    picked = picked * mine.astype(jnp.float32)[:, None]
    compact_keys = lax.psum(picked, "ctx").astype(jnp.bfloat16)
    attend = compact_softmax(queries_ref, compact_keys, score_scale)
    gram = inner_left(attend, attend)
    cross = inner_left(attend, target)
    ridge = ridge_share * jnp.trace(gram) / M
    system = gram + ridge * jnp.eye(M, dtype=jnp.float32)
    factor_low = jnp.linalg.cholesky(system)
    halfway = lax.linalg.triangular_solve(factor_low, cross, left_side=True, lower=True)
    compact = lax.linalg.triangular_solve(
        factor_low, halfway, left_side=True, lower=True, transpose_a=True
    )
    target_square = jnp.sum(target * target)
    fitted_square = jnp.sum(
        compact
        * jnp.dot(
            gram, compact, precision=lax.Precision.HIGHEST, preferred_element_type=jnp.float32
        )
    )
    head_error = (target_square - 2.0 * jnp.sum(compact * cross) + fitted_square) / target_square
    fit_error = lax.psum(head_error, "head") / lax.axis_size("head")
    return (compact[None], fit_error)


def solution(mesh):
    placed = (
        P("head", "ctx", None, None),
        P("head", "ctx", None),
        P("head", "ctx", None),
        P("head", None),
        P("head"),
    )
    return jax.shard_map(
        per_device,
        mesh=mesh,
        in_specs=placed,
        out_specs=(P("head", None, None), P()),
        check_vma=False,
    )
```

profile of v0, /device:TPU:1, one launch (start us, length us, event | category | flops | bytes accessed | tf_op | source)
XLA Modules:
  0.0 929.7 jit_solution(15579256206267281522)
XLA Ops:
  12.7 260.3 %all-reduce.6.cloned.1.call-done = bf16[1024,128]{1,0:T(8,128)(2,1)} async-done(((bf16[1024,128]{1,0:T(8,128)(2,1)}), bf16[1024,128]{1,0:T(8,128)(2,1)}) %all-reduce.6.cloned.1.call-update) | async-done | bytes 262160 | tf_op jit(solution)/shard_map/psum | solution.py:18
  273.0 31.4 %while.17 = (s32[]{:T(128)}, f32[1024]{0:T(1024)S(1)}, f32[1024]{0:T(1024)S(1)}, f32[1024,128]{1,0:T(8,128)S(1)}, bf16[4,1024,128]{2,1,0:T(8,128)(2,1)}, /*index...) while((s32[]{:T(128)}, f32[1024]{0:T(1024)S(1)}, ...), condition=%wide.region_16.17_spmd.clone, body=%wide.region_13.16_spmd.clone.sunk | while | flops 547887104 | bytes 31252628 | solution.py:57
  277.4 3.4 fusion.100
  285.3 3.4 fusion.100
  293.1 3.4 fusion.100
  301.0 3.4 fusion.100
  304.4 113.1 %pmax.7 = f32[1024]{0:T(1024)S(1)} all-reduce(f32[1024]{0:T(1024)S(1)} %get-tuple-element.42), channel_id=1, replica_groups=mesh['head'=8,'ctx'=64] {'ctx'}, use_global_device_ids=true, to_apply=%region_17.18 | all-reduce | flops 1024 | bytes 8192 | tf_op jit(solution)/shard_map/pmax | solution.py:82
  418.5 222.3 %all-reduce.9 = (bf16[512,128]{1,0:T(8,128)(2,1)S(1)}, f32[1024]{0:T(1024)S(1)}) all-reduce(f32[512,128]{1,0:T(8,128)S(1)} %convert_multiply_fusion, f32[1024]{0:T(1024)S(1)} %get-tuple-element.104), channel_id=1, replica_groups=mesh['head'=8,'ctx'=64] {'ctx'}, use_global_device_ids=true, to_apply=%region_1.2 | all-reduce | flops 66560 | bytes 401408 | tf_op jit(solution)/shard_map/psum | solution.py:94
  642.6 4.7 select_reduce_fusion
  651.8 11.7 %cholesky.103 = f32[128,128]{1,0:T(8,128)S(1)} custom-call(f32[128,128]{1,0:T(8,128)S(1)} %cholesky.263), custom_call_target="Cholesky" | custom-call | tf_op jit(solution)/shard_map/jit(cholesky)/cholesky | solution.py:100
  664.7 9.8 %custom-call.32 = f32[1,128,128]{1,2,0:T(8,128)S(1)} custom-call(f32[1,128,128]{2,1,0:T(8,128)S(1)} %get-tuple-element.121), custom_call_target="InvertDiagBlocksLowerTriangular" | custom-call | tf_op jit(solution)/shard_map/jit(cholesky)/cholesky | solution.py:100
  677.7 12.2 %cholesky.215 = f32[128,128]{1,0:T(8,128)S(1)} custom-call(f32[128,128]{1,0:T(8,128)S(1)} %cholesky.267), custom_call_target="Cholesky" | custom-call | tf_op jit(solution)/shard_map/jit(cholesky)/cholesky | solution.py:100
  690.6 9.8 %custom-call.33 = f32[1,128,128]{1,2,0:T(8,128)S(1)} custom-call(f32[1,128,128]{2,1,0:T(8,128)S(1)} %get-tuple-element.118), custom_call_target="InvertDiagBlocksLowerTriangular" | custom-call | tf_op jit(solution)/shard_map/jit(cholesky)/cholesky | solution.py:100
  702.8 11.7 %cholesky.236 = f32[128,128]{1,0:T(8,128)S(1)} custom-call(f32[128,128]{1,0:T(8,128)S(1)} %cholesky.272), custom_call_target="Cholesky" | custom-call | tf_op jit(solution)/shard_map/jit(cholesky)/cholesky | solution.py:100
  715.1 9.8 %custom-call.34 = f32[1,128,128]{1,2,0:T(8,128)S(1)} custom-call(f32[1,128,128]{2,1,0:T(8,128)S(1)} %get-tuple-element.115), custom_call_target="InvertDiagBlocksLowerTriangular" | custom-call | tf_op jit(solution)/shard_map/jit(cholesky)/cholesky | solution.py:100
  727.4 11.7 %cholesky.253 = f32[128,128]{1,0:T(8,128)S(1)} custom-call(f32[128,128]{1,0:T(8,128)S(1)} %convolution_subtract_fusion.8), custom_call_target="Cholesky" | custom-call | tf_op jit(solution)/shard_map/jit(cholesky)/cholesky | solution.py:100
  746.6 14.4 %while.16 = (s32[]{:T(128)}, f32[512,512]{1,0:T(8,128)}, s32[4,2]{0,1:T(2,128)S(1)}, f32[4,128,128]{2,1,0:T(8,128)}, s32[]{:T(128)}) while((s32[]{:T(128)}, f32[512,512]{1,0:T(8,128)}, s32[4,2]{0,1:T(2,128)S(1)}, f32[4,128,128]{2,1,0:T(8,128)}, s32[]{:T(128)}) %tuple.64), condition=%wide.while_cond, body=%wide.while_body.sunk | while | flops 2 | bytes 132205 | solution.py:102
  747.3 3.0 bitcast_dynamic-update-slice_fusion.2
  750.9 3.0 bitcast_dynamic-update-slice_fusion.2
  754.6 3.0 bitcast_dynamic-update-slice_fusion.2
  758.2 2.9 bitcast_dynamic-update-slice_fusion.2
  761.1 40.3 %custom-call.35 = f32[4,128,128]{1,2,0:T(8,128)S(1)} custom-call(f32[4,128,128]{2,1,0:T(8,128)} %get-tuple-element.51), custom_call_target="InvertDiagBlocksLowerTriangular" | custom-call | tf_op jit(solution)/shard_map/triangular_solve | solution.py:102
  801.4 3.2 fusion.15
  815.1 105.7 %psum.39 = f32[]{:T(128)} all-reduce(f32[]{:T(128)S(6)} %div.56), channel_id=1, replica_groups=mesh['head'=8,'ctx'=64] {'head'}, use_global_device_ids=true, to_apply=%region_23.24 | all-reduce | flops 1 | bytes 8 | tf_op jit(solution)/shard_map/psum | solution.py:113
  (92 shorter events, 55.0 us)
Async XLA Ops:
  7.2 265.8 %all-reduce.6.cloned.1.call-start = ((), (), s32[]{:S(2)}) async-start(), calls=%async_computation | async-start | bytes 524288 | tf_op jit(solution)/shard_map/psum | solution.py:18
  8.6 792.8 %all-reduce.8.cloned.1.call-start = ((), (), s32[]{:S(2)}) async-start(), calls=%async_computation.1 | async-start | bytes 1048576 | tf_op jit(solution)/shard_map/psum | solution.py:84
  274.7 1.9 copy-start
  282.6 1.9 copy-start
  290.4 1.9 copy-start
  298.3 1.9 copy-start
  650.7 1.0 copy-start.2
  801.4 3.5 copy-start.1
  806.3 6.0 copy-start.3
Sparse Core Ops, SparseCore 0:
  12.0 260.9 all-reduce.5
  418.6 285.3 all-reduce.7
where the time goes:
time: 934 us; the launch traced here: 930 us
  blocking collectives  441 us (47%)
  waiting for transfers between devices  260 us (28%)
  other arithmetic  134 us (14%)
  matrix products  43.4 us (5%)
  local copies, waits for them, and re-layouts  28 us (3%)
  between operations  22.9 us (2%)
    psum x1, waiting for transfers between devices, spread(): return lax.psum(jnp.where(mine, array, jnp.zeros_like(array)), axis)  260 us
    psum x1, blocking collectives, per_device(): compact_keys = lax.psum(picked, 'ctx').astype(jnp.bfloat16)  222 us
    pmax x1, blocking collectives, per_device(): highest = lax.pmax(run_max, 'ctx')  113 us
    psum x1, blocking collectives, per_device(): fit_error = lax.psum(head_error, 'head') / lax.axis_size('head')  106 us
    another operation x14, other arithmetic, per_device(): factor_low = jnp.linalg.cholesky(system)  80.8 us
    another operation x3, other arithmetic, per_device(): lax.linalg.triangular_solve(factor_low, halfway, left_side=True, lower=Tr...  42.7 us
  transfers between devices with their start and end apart: 2, of which 1 were waited for; matrix products, arithmetic and copies ran while one was open for 17% of the time, Pallas kernels for 0%

commit v1 on v0

v1 whole, which is shorter than its diff:
```python
import math

import jax
import jax.numpy as jnp
from jax import lax
from jax.experimental import pallas as pl
from jax.experimental.pallas import tpu as pltpu
from jax.sharding import PartitionSpec as P

HD = 128
KBLK = 1024
M = 512
NY = 4
NZ = 16
NHEAD = 8
SLAB = 4096
QC = 256
CC = 128
PAY = QC + CC
NSUB = 3
SUB = PAY // NSUB
BLK = 128
SCALE = 1.0 / math.sqrt(HD)
RIDGE = 0.01
F32 = jnp.float32
BF16 = jnp.bfloat16
HIGHEST = lax.Precision.HIGHEST
MESH = pl.DeviceIdType.MESH


def dotf(a, b, ca, cb, precision=None):
    return lax.dot_general(
        a, b, (((ca,), (cb,)), ((), ())), precision=precision, preferred_element_type=F32
    )


def invert_block(tiles):
    lane = lax.broadcasted_iota(jnp.int32, (8, BLK), 1)
    sub = lax.broadcasted_iota(jnp.int32, (8, BLK), 0)

    def group(_, carry):
        t = list(carry)
        for j in range(8):
            hit = lane == j
            own = sub == j
            pivot = t[0][j : j + 1, j : j + 1]
            inv = 1.0 / jnp.broadcast_to(pivot, (8, BLK))
            row = jnp.broadcast_to(t[0][j : j + 1, :], (8, BLK)) * inv
            row = jnp.where(hit, inv, row)
            cols = [jnp.broadcast_to(x[:, j : j + 1], (8, BLK)) for x in t]
            fresh = [jnp.where(hit, 0.0, x) - c * row for x, c in zip(t, cols)]
            fresh[0] = jnp.where(own, row, fresh[0])
            t = fresh
        t = t[1:] + t[:1]
        return tuple(pltpu.roll(x, BLK - 8, 1) for x in t)

    return lax.fori_loop(0, BLK // 8, group, tuple(tiles))


def sweep_block(s_ref, b):
    lo = b * BLK
    tiles = [s_ref[lo + 8 * i : lo + 8 * i + 8, lo : lo + BLK] for i in range(16)]
    inv = jnp.concatenate(invert_block(tiles), axis=0)
    old = s_ref[lo : lo + BLK, :]
    row = dotf(inv, old, 1, 0, HIGHEST)
    s_ref[lo : lo + BLK, :] = row
    s_ref[lo : lo + BLK, lo : lo + BLK] = inv
    for i in range(M // BLK):
        if i == b:
            continue
        r0 = i * BLK
        col = s_ref[r0 : r0 + BLK, lo : lo + BLK]
        s_ref[r0 : r0 + BLK, lo : lo + BLK] = jnp.zeros((BLK, BLK), F32)
        s_ref[r0 : r0 + BLK, :] -= dotf(col, s_ref[lo : lo + BLK, :], 1, 0, HIGHEST)


def body(
    q_hbm, k_hbm, v_hbm, kept_ref, roots_ref, out_ref, fit_ref,
    q_ref, k_ref, v_ref, vt_ref, pm, rq, fl_own, fl_r, fl_l, qall, cfull,
    osend, orecv, comb, ml_own, rz_o, rz_ml, yown, ybuf, at, s_ref, fit_own, fit_in,
    ld_sem, rq_ss, rq_rs, fr_ss, fr_rs, fl_ss, fl_rs, aq_ss, aq_rs, ac_ss, ac_rs,
    o_ss, o_rs, z_ss, z_rs, m_ss, m_rs, g_ss, g_rs, y_ss, y_rs, h_ss, h_rs,
):
    head = lax.axis_index("head")
    ctx = lax.axis_index("ctx")
    y = ctx // NZ
    z = ctx % NZ

    def at_y(d):
        return (head, ((y + d) % NY) * NZ + z)

    def at_z(t):
        return (head, y * NZ + (z + t) % NZ)

    def at_h(g):
        return ((head + g) % NHEAD, ctx)

    def send(src, dst, ss, rs, dev):
        copy = pltpu.make_async_remote_copy(
            src_ref=src, dst_ref=dst, send_sem=ss, recv_sem=rs, device_id=dev, device_id_type=MESH
        )
        copy.start()
        return copy

    def desc(src, dst, ss, rs):
        return pltpu.make_async_remote_copy(
            src_ref=src, dst_ref=dst, send_sem=ss, recv_sem=rs, device_id=at_z(1), device_id_type=MESH
        )

    ld_q = pltpu.make_async_copy(q_hbm, q_ref, ld_sem.at[0])
    ld_k = pltpu.make_async_copy(k_hbm, k_ref, ld_sem.at[1])
    ld_v = pltpu.make_async_copy(v_hbm, v_ref, ld_sem.at[2])
    ld_q.start()
    ld_k.start()
    ld_v.start()

    barrier = pltpu.get_barrier_semaphore()
    peers = [at_y(1), at_y(2), at_y(3), at_z(1), at_z(NZ - 1)] + [at_h(g) for g in range(1, NHEAD)]
    for dev in peers:
        pl.semaphore_signal(barrier, inc=1, device_id=dev, device_id_type=MESH)

    pending = []

    ld_q.wait()
    mine = jnp.broadcast_to(roots_ref[0], (QC, HD)) == ctx
    for i in range(NY):
        part = q_ref[i * QC : (i + 1) * QC, :].astype(F32)
        pm[i, 0:QC, :] = jnp.where(mine, part, 0.0).astype(BF16)
    pl.semaphore_wait(barrier, len(peers))
    for d in (2, 1, 3):
        to = (y + d) % NY
        pending.append(
            send(pm.at[to, pl.ds(0, QC)], rq.at[d - 1, pl.ds(0, QC)],
                 rq_ss.at[d - 1, 0], rq_rs.at[d - 1, 0], at_y(d))
        )

    ld_k.wait()
    base = (ctx * SLAB).astype(F32)
    kept_t = jnp.transpose(jnp.broadcast_to(kept_ref[...].astype(F32), (BLK, M))) - base
    lane = lax.broadcasted_iota(jnp.int32, (M, BLK), 1).astype(F32)
    s_ref[:, 0:HD] = jnp.zeros((M, HD), F32)

    def pick(c, _):
        first = kept_t - (c * (2 * BLK)).astype(F32)
        a = jnp.where(first == lane, 1.0, 0.0).astype(BF16)
        b = jnp.where(first == lane + float(BLK), 1.0, 0.0).astype(BF16)
        rows = k_ref[pl.ds(pl.multiple_of(c * (2 * BLK), 2 * BLK), 2 * BLK), :]
        s_ref[:, 0:HD] += dotf(jnp.concatenate([a, b], axis=1), rows, 1, 0)
        return 0

    lax.fori_loop(0, SLAB // (2 * BLK), pick, 0)
    for i in range(NY):
        pm[i, QC:PAY, :] = s_ref[i * CC : (i + 1) * CC, 0:HD].astype(BF16)
    for d in (2, 1, 3):
        to = (y + d) % NY
        pending.append(
            send(pm.at[to, pl.ds(QC, CC)], rq.at[d - 1, pl.ds(QC, CC)],
                 rq_ss.at[d - 1, 1], rq_rs.at[d - 1, 1], at_y(d))
        )

    ld_v.wait()
    vt_ref[HD : HD + 16, :] = jnp.ones((16, SLAB), BF16)
    for i in range(SLAB // 512):
        piece = v_ref[i * 512 : (i + 1) * 512, :].astype(F32)
        vt_ref[0:HD, i * 512 : (i + 1) * 512] = jnp.transpose(piece).astype(BF16)

    def gathered(part, lo, size):
        for d in range(1, NY):
            desc(pm.at[0, pl.ds(lo, size)], rq.at[d - 1, pl.ds(lo, size)],
                 rq_ss.at[d - 1, part], rq_rs.at[d - 1, part]).wait_recv()
        total = pm[y, lo : lo + size, :].astype(F32)
        for d in range(1, NY):
            total = total + rq[d - 1, lo : lo + size, :].astype(F32)
        fl_own[lo : lo + size, :] = total.astype(BF16)

    right = at_z(1)
    left = at_z(NZ - 1)
    steps_r, steps_l = NZ // 2, NZ // 2 - 1

    def forward_r(t, u):
        rows = pl.ds(u * SUB, SUB)
        src = fl_own.at[rows] if t == 0 else fl_r.at[t - 1, rows]
        pending.append(send(src, fl_r.at[t, rows], fr_ss.at[t, u], fr_rs.at[t, u], right))

    def forward_l(t, u):
        rows = pl.ds(u * SUB, SUB)
        src = fl_own.at[rows] if t == 0 else fl_l.at[t - 1, rows]
        pending.append(send(src, fl_l.at[t, rows], fl_ss.at[t, u], fl_rs.at[t, u], left))

    gathered(0, 0, QC)
    for u in range(2):
        forward_r(0, u)
        forward_l(0, u)
    gathered(1, QC, CC)
    forward_r(0, 2)
    forward_l(0, 2)
    for t in range(steps_r):
        for u in range(NSUB):
            rows = pl.ds(u * SUB, SUB)
            desc(fl_own.at[rows], fl_r.at[t, rows], fr_ss.at[t, u], fr_rs.at[t, u]).wait_recv()
            if t + 1 < steps_r:
                forward_r(t + 1, u)
            if t < steps_l:
                desc(fl_own.at[rows], fl_l.at[t, rows], fl_ss.at[t, u], fl_rs.at[t, u]).wait_recv()
                if t + 1 < steps_l:
                    forward_l(t + 1, u)

    def summed(lo, size):
        total = fl_own[lo : lo + size, :].astype(F32)
        for t in range(steps_r):
            total = total + fl_r[t, lo : lo + size, :].astype(F32)
        for t in range(steps_l):
            total = total + fl_l[t, lo : lo + size, :].astype(F32)
        return total.astype(BF16)

    qall[0] = summed(0, QC)
    for d in (1, 3, 2):
        pending.append(send(qall.at[0], qall.at[d], aq_ss.at[d - 1], aq_rs.at[d - 1], at_y(NY - d)))
    mine_c = pl.ds(pl.multiple_of(y * CC, CC), CC)
    cfull[mine_c, :] = summed(QC, CC)
    for d in (1, 3, 2):
        pending.append(
            send(cfull.at[mine_c], cfull.at[mine_c], ac_ss.at[d - 1], ac_rs.at[d - 1], at_y(NY - d))
        )

    for d in (0, 1, 3, 2):
        if d:
            desc(qall.at[0], qall.at[d], aq_ss.at[d - 1], aq_rs.at[d - 1]).wait_recv()
        qd = qall[d]
        top, acc = None, None
        for b in range(SLAB // KBLK):
            s = dotf(k_ref[b * KBLK : (b + 1) * KBLK, :], qd, 1, 1)
            high = jnp.max(s, axis=0, keepdims=True) * SCALE
            e = jnp.exp(s * SCALE - high).astype(BF16)
            o = dotf(vt_ref[:, b * KBLK : (b + 1) * KBLK], e, 1, 0)
            if b == 0:
                top, acc = high, o
            else:
                joint = jnp.maximum(top, high)
                acc = acc * jnp.exp(top - joint) + o * jnp.exp(high - joint)
                top = joint
        osend[d, 0 : HD + 8, :] = acc[0 : HD + 8]
        osend[d, HD + 8 : HD + 16, :] = jnp.broadcast_to(top, (8, QC))
        if d:
            pending.append(send(osend.at[d], orecv.at[d - 1], o_ss.at[d - 1], o_rs.at[d - 1], at_y(d)))

    for d in (1, 3, 2):
        desc(cfull.at[mine_c], cfull.at[mine_c], ac_ss.at[d - 1], ac_rs.at[d - 1]).wait_recv()
    for d in range(NY):
        s = dotf(cfull[...], qall[d], 1, 1) * SCALE
        e = jnp.exp(s - jnp.max(s, axis=0, keepdims=True))
        at[d] = e / jnp.sum(e, axis=0, keepdims=True)

    for d in range(1, NY):
        desc(osend.at[d], orecv.at[d - 1], o_ss.at[d - 1], o_rs.at[d - 1]).wait_recv()
    tops = [osend[0, HD + 8 : HD + 9, :]] + [orecv[d, HD + 8 : HD + 9, :] for d in range(NY - 1)]
    joint = jnp.maximum(jnp.maximum(tops[0], tops[1]), jnp.maximum(tops[2], tops[3]))
    total = osend[0, 0 : HD + 8, :] * jnp.exp(tops[0] - joint)
    for d in range(NY - 1):
        total = total + orecv[d, 0 : HD + 8, :] * jnp.exp(tops[d + 1] - joint)
    comb[...] = total[0:HD]
    ml_own[0:1, 0:QC] = total[HD : HD + 1]
    ml_own[0:1, QC : 2 * QC] = joint

    def z_rows(t):
        return pl.ds(pl.multiple_of(((z + t) % NZ) * 8, 8), 8)

    for t in sorted(range(1, NZ), key=lambda t: -min(t, NZ - t)):
        pending.append(send(comb.at[z_rows(t)], rz_o.at[t - 1], z_ss.at[t - 1], z_rs.at[t - 1], at_z(t)))
        pending.append(send(ml_own, rz_ml.at[t - 1], m_ss.at[t - 1], m_rs.at[t - 1], at_z(t)))

    def gram(i, _):
        rows = pl.ds(pl.multiple_of(i * BLK, BLK), BLK)
        total = dotf(at[0, rows, :], at[0], 1, 1, HIGHEST)
        for d in range(1, NY):
            total = total + dotf(at[d, rows, :], at[d], 1, 1, HIGHEST)
        s_ref[rows, :] = total
        return 0

    lax.fori_loop(0, M // BLK, gram, 0)
    eye = lax.broadcasted_iota(jnp.int32, (M, M), 0) == lax.broadcasted_iota(jnp.int32, (M, M), 1)
    trace = jnp.sum(jnp.where(eye, s_ref[...], 0.0), keepdims=True)
    s_ref[...] += jnp.where(eye, trace * (RIDGE / M), 0.0)
    sweep_block(s_ref, 0)

    for t in range(1, NZ):
        desc(comb.at[z_rows(0)], rz_o.at[t - 1], z_ss.at[t - 1], z_rs.at[t - 1]).wait_recv()
        desc(ml_own, rz_ml.at[t - 1], m_ss.at[t - 1], m_rs.at[t - 1]).wait_recv()
    joint = ml_own[0:1, QC : 2 * QC]
    for t in range(NZ - 1):
        joint = jnp.maximum(joint, rz_ml[t, 0:1, QC : 2 * QC])
    w = jnp.exp(ml_own[0:1, QC : 2 * QC] - joint)
    total = comb[z_rows(0), :] * w
    weight = ml_own[0:1, 0:QC] * w
    for t in range(NZ - 1):
        w = jnp.exp(rz_ml[t, 0:1, QC : 2 * QC] - joint)
        total = total + rz_o[t] * w
        weight = weight + rz_ml[t, 0:1, 0:QC] * w
    ybuf[0, z_rows(0), :] = total / weight
    far = sorted(range(1, NZ), key=lambda t: -min(t, NZ - t))
    for t in far:
        pending.append(
            send(ybuf.at[0, z_rows(0)], ybuf.at[0, z_rows(0)], g_ss.at[t - 1], g_rs.at[t - 1], at_z(t))
        )

    def relay(t):
        rows = z_rows(NZ - t)
        for d in range(1, NY):
            pending.append(
                send(ybuf.at[0, rows], ybuf.at[d, rows], y_ss.at[d - 1, t], y_rs.at[d - 1, t], at_y(NY - d))
            )

    relay(0)
    sweep_block(s_ref, 1)
    sweep_block(s_ref, 2)
    for t in reversed(far):
        desc(ybuf.at[0, z_rows(0)], ybuf.at[0, z_rows(NZ - t)], g_ss.at[t - 1], g_rs.at[t - 1]).wait_recv()
        relay(t)
    sweep_block(s_ref, 3)
    for t in range(NZ):
        for d in range(1, NY):
            rows = z_rows(NZ - t)
            desc(ybuf.at[0, rows], ybuf.at[d, rows], y_ss.at[d - 1, t], y_rs.at[d - 1, t]).wait_recv()

    cross = dotf(at[0], ybuf[0], 1, 1, HIGHEST)
    for d in range(1, NY):
        cross = cross + dotf(at[d], ybuf[d], 1, 1, HIGHEST)
    compact = dotf(s_ref[...], cross, 1, 0, HIGHEST)
    out_ref[...] = compact
    misfit = jnp.zeros((1, 1), F32)
    norm = jnp.zeros((1, 1), F32)
    compact_t = jnp.transpose(compact)
    for d in range(NY):
        target = ybuf[d]
        off = dotf(compact_t, at[d], 1, 0, HIGHEST) - target
        misfit = misfit + jnp.sum(off * off, keepdims=True)
        norm = norm + jnp.sum(target * target, keepdims=True)
    fit_own[...] = jnp.broadcast_to(misfit / norm, (8, 128))
    for g in range(1, NHEAD):
        pending.append(send(fit_own, fit_in.at[g - 1], h_ss.at[g - 1], h_rs.at[g - 1], at_h(g)))
    for g in range(1, NHEAD):
        desc(fit_own, fit_in.at[g - 1], h_ss.at[g - 1], h_rs.at[g - 1]).wait_recv()
    total = fit_own[...]
    for g in range(NHEAD - 1):
        total = total + fit_in[g]
    fit_ref[...] = total * (1.0 / NHEAD)
    for copy in pending:
        copy.wait_send()


def per_device(queries, keys, values, kept, roots):
    dma = pltpu.SemaphoreType.DMA
    anywhere = pl.BlockSpec(memory_space=pl.ANY)
    vmem = pl.BlockSpec(memory_space=pltpu.VMEM)
    compact, fit = pl.pallas_call(
        body,
        name="compaction",
        out_shape=(jax.ShapeDtypeStruct((M, HD), F32), jax.ShapeDtypeStruct((8, 128), F32)),
        in_specs=[anywhere, anywhere, anywhere, vmem, pl.BlockSpec(memory_space=pltpu.SMEM)],
        out_specs=(vmem, vmem),
        scratch_shapes=[
            pltpu.VMEM((NY * QC, HD), BF16),
            pltpu.VMEM((SLAB, HD), BF16),
            pltpu.VMEM((SLAB, HD), BF16),
            pltpu.VMEM((HD + 16, SLAB), BF16),
            pltpu.VMEM((NY, PAY, HD), BF16),
            pltpu.VMEM((NY - 1, PAY, HD), BF16),
            pltpu.VMEM((PAY, HD), BF16),
            pltpu.VMEM((NZ // 2, PAY, HD), BF16),
            pltpu.VMEM((NZ // 2 - 1, PAY, HD), BF16),
            pltpu.VMEM((NY, QC, HD), BF16),
            pltpu.VMEM((M, HD), BF16),
            pltpu.VMEM((NY, HD + 16, QC), F32),
            pltpu.VMEM((NY - 1, HD + 16, QC), F32),
            pltpu.VMEM((HD, QC), F32),
            pltpu.VMEM((1, 2 * QC), F32),
            pltpu.VMEM((NZ - 1, 8, QC), F32),
            pltpu.VMEM((NZ - 1, 1, 2 * QC), F32),
            pltpu.VMEM((8, QC), F32),
            pltpu.VMEM((NY, HD, QC), F32),
            pltpu.VMEM((NY, M, QC), F32),
            pltpu.VMEM((M, M), F32),
            pltpu.VMEM((8, 128), F32),
            pltpu.VMEM((NHEAD - 1, 8, 128), F32),
            dma((3,)),
            dma((NY - 1, 2)), dma((NY - 1, 2)),
            dma((NZ // 2, NSUB)), dma((NZ // 2, NSUB)),
            dma((NZ // 2 - 1, NSUB)), dma((NZ // 2 - 1, NSUB)),
            dma((NY - 1,)), dma((NY - 1,)),
            dma((NY - 1,)), dma((NY - 1,)),
            dma((NY - 1,)), dma((NY - 1,)),
            dma((NZ - 1,)), dma((NZ - 1,)),
            dma((NZ - 1,)), dma((NZ - 1,)),
            dma((NZ - 1,)), dma((NZ - 1,)),
            dma((NY - 1, NZ)), dma((NY - 1, NZ)),
            dma((NHEAD - 1,)), dma((NHEAD - 1,)),
        ],
        compiler_params=pltpu.CompilerParams(
            collective_id=0, has_side_effects=True, vmem_limit_bytes=60 * 1024 * 1024
        ),
    )(queries[0, 0], keys[0], values[0], kept, roots)
    return (compact[None], fit[0, 0])


def solution(mesh):
    placed = (
        P("head", "ctx", None, None),
        P("head", "ctx", None),
        P("head", "ctx", None),
        P("head", None),
        P("head"),
    )
    return jax.shard_map(
        per_device,
        mesh=mesh,
        in_specs=placed,
        out_specs=(P("head", None, None), P()),
        check_vma=False,
    )
```

time: 934 us -> 164 us (0.18)
  blocking collectives: 441 us -> 0 us
  waiting for transfers between devices: 260 us -> 0 us
  Pallas kernels: 0 us -> 160 us
  other arithmetic: 134 us -> 0 us
  matrix products: 43.4 us -> 0 us
  local copies, waits for them, and re-layouts: 28 us -> 2.86 us
  between operations: 22.9 us -> 1.29 us
    psum x2 -> x0, blocking collectives: 328 us -> none  [the longest x1 222 us: per_device(): compact_keys = lax.psum(picked, 'ctx').astype(jnp.bfloat16)]
    psum x2 -> x0, waiting for transfers between devices: 260 us -> none  [the longest x1 260 us: spread(): return lax.psum(jnp.where(mine, array, jnp.zeros_like(array)), axis)]
    pallas_call x0 -> x1, Pallas kernels: none -> 160 us  [per_device(): pl.pallas_call(body, name='compaction', out_shape=(jax.ShapeDtypeStruct((...]
    another operation x17 -> x0, other arithmetic: 123 us -> none  [the longest x14 80.8 us: per_device(): factor_low = jnp.linalg.cholesky(system)]
    pmax x1 -> x0, blocking collectives: 113 us -> none  [per_device(): highest = lax.pmax(run_max, 'ctx')]
    dot_general x12 -> x0, matrix products: 31.5 us -> none  [the longest x4 13.6 us: visit(): jnp.dot(weights, value_block, preferred_element_type=jnp.float32)]
    another operation x17 -> x0, local copies, waits for them, and re-layouts: 15.6 us -> none
    another operation x20 -> x0, matrix products: 11.9 us -> none  [the longest x6 7.98 us: per_device(): factor_low = jnp.linalg.cholesky(system)]
  transfers between devices with their start and end apart: 2 -> 0, of which waited for: 1 -> 0; matrix products, arithmetic and copies ran while one was open for 17% -> 0% of each run, Pallas kernels for 0% -> 0%
where the time goes in v1:
time: 164 us
  Pallas kernels  160 us (98%)
  local copies, waits for them, and re-layouts  2.86 us (2%)
    pallas_call x1, Pallas kernels, per_device(): pl.pallas_call(body, name='compaction', out_shape=(jax.ShapeDtypeStruct((...  160 us

profile of v1, /device:TPU:1, one launch (start us, length us, event | category | flops | bytes accessed | tf_op | source)
XLA Modules:
  0.0 163.7 jit_solution(12071992345552930808)
XLA Ops:
  1.3 159.5 %compaction.1 = (f32[512,128]{1,0:T(8,128)}, f32[8,128]{1,0:T(8,128)}) custom-call(bf16[1024,128]{1,0:T(8,128)(2,1)} %bitcast.7, bf16[4096,128]{1,0:T(8,128)(2,1)} %bitcast.5, bf16[4096,128]{1,0:T(8,128)(2,1)} %bitcast.6, s32[1,512]{1,0:T(1,128)} %kept_ref.1, s32[1]{0:T(128)S(6)} %copy.8.roots_ref), custom_call_target="tpu_custom_call" | custom-call | tf_op jit(solution)/shard_map/compaction/pallas_call | solution.py:355
  160.8 1.2 slice.3
  162.0 1.7 %copy.9 = f32[1,512,128]{2,1,0:T(8,128)} copy(f32[1,512,128]{2,1,0:T(8,128)} %bitcast.8) | data formatting | bytes 524288
